TPU v7x, 256 devices: a whole 4x4x8 slice. The times are simulated.
256 devices in a mesh: user: 16 (over z, core), item: 16 (over y, x).
Axes of the slice: x: 4, y: 4, z: 8, core: 2. Of those that a mesh axis runs over, the one named last changes fastest.
Arguments:
- user_factors: float32 [8192, 256], P('user'), may hold values from -0.3 to 0.3, as said below
- item_factors: float32 [8192, 256], P('item'), may hold values from -0.6 to 0.6
- tile_user: int32 [16, 16, 16, 2], P('item', 'user'), may hold values from 0 to 3
- tile_item: int32 [16, 16, 16, 2], P('item', 'user'), may hold values from 0 to 3
- tile_count: int32 [16, 16, 16], P('item', 'user'), may hold values from 1 to 2, as said below
- tile_conf: bfloat16 [16, 16, 16, 2, 128, 128], P('item', 'user'), may hold values from 0.099609375 to 4
- held_user: int32 [16, 16, 16, 2], P('user', 'item'), may hold values from 0 to 1
- held_item: int32 [16, 16, 16, 2], P('user', 'item'), may hold values from 0 to 3
- held_count: int32 [16, 16, 16], P('user', 'item'), may hold values from 1 to 2, as said below
- held_conf: bfloat16 [16, 16, 16, 2, 128, 128], P('user', 'item'), may hold values from 0.099609375 to 4
Outputs:
- new_items: float32 [8192, 256], P('item')
- folded_users: float32 [4096, 256], P('user')
Inputs may be any that keep to these rules, and one draw needn't show every extreme that they name: `user_factors`: user factors; the scale of a factor column varies by up to a factor of ten. `tile_count`: some device has an owner with all 2 slots live and one with a single live slot. `held_count`: some device has an owner with all 2 slots live and one with a single live slot.
All inputs are finite; a program needn't handle non-finite values.
Results may differ from a plain program's by a relative error of at most 0.0003.
Values may be sent and summed in bfloat16 or wider, within the bound.
No kernel may reach another device: no remote copies, remote signals or barrier semaphores. Data moves between devices by JAX's collectives and lax.ppermute only.
A program may use at most 128 MiB of HBM per device.

v0:
```python
import jax
import jax.numpy as jnp
from jax import lax
from jax.sharding import PartitionSpec as P

HB_DEV = 2
ITERS = 2
highest = lax.Precision.HIGHEST
ridge_weight = 1.0
epsilon = 1e-06


def local_gram(rows):
    return jnp.einsum("nk,nm->km", rows, rows, precision=highest)


def gram_apply(vector, gram):
    return jnp.einsum("jck,km->jcm", vector, gram, precision=highest) + ridge_weight * vector


def block_onehot(positions, blocks):
    return (positions[:, None] == jnp.arange(blocks, dtype=jnp.int32)[None, :]).astype(jnp.float32)


def item_terms(factors, weights, positions, onehot, vector):
    picked = vector[positions]
    scores = jnp.einsum("tuk,tik->tui", factors, picked, precision=highest) * weights
    terms = jnp.einsum("tui,tuk->tik", scores, factors, precision=highest)
    return jnp.einsum("tj,tik->jik", onehot, terms, precision=highest)


def item_right(factors, right_weights, onehot):
    terms = jnp.einsum("tui,tuk->tik", right_weights, factors, precision=highest)
    return jnp.einsum("tj,tik->jik", onehot, terms, precision=highest)


def held_terms(factors, weights, positions, onehot, vector):
    picked = vector[positions]
    scores = jnp.einsum("tik,thk->thi", factors, picked, precision=highest) * weights
    terms = jnp.einsum("thi,tik->thk", scores, factors, precision=highest)
    return jnp.einsum("tj,thk->jhk", onehot, terms, precision=highest)


def held_right(factors, right_weights, onehot):
    terms = jnp.einsum("thi,tik->thk", right_weights, factors, precision=highest)
    return jnp.einsum("tj,thk->jhk", onehot, terms, precision=highest)


def conjugate(operator, residual, start):
    solution = start
    direction = residual
    norm_now = jnp.sum(residual * residual, axis=-1, keepdims=True)
    for iteration in range(ITERS):
        image = operator(direction)
        alpha = norm_now / (jnp.sum(direction * image, axis=-1, keepdims=True) + epsilon)
        solution = solution + alpha * direction
        residual = residual - alpha * image
        norm_next = jnp.sum(residual * residual, axis=-1, keepdims=True)
        direction = residual + norm_next / (norm_now + epsilon) * direction
        norm_now = norm_next
    return solution


def user_total(partial_value):
    return lax.psum(partial_value, "user")


def item_total(partial_value):
    return lax.psum(partial_value, "item")


def tile_weights(confidence, live_slots, tile_width):
    live_flat = live_slots.reshape(-1).astype(jnp.float32)[:, None, None]
    conf_flat = confidence.reshape(-1, tile_width, tile_width).astype(jnp.float32)
    return (conf_flat * live_flat, (1.0 + conf_flat) * live_flat)


def shards(
    user_factors,
    item_factors,
    tile_user,
    tile_item,
    tile_count,
    tile_conf,
    held_user,
    held_item,
    held_count,
    held_conf,
):
    factor_rank = user_factors.shape[1]
    tile_width = tile_conf.shape[-1]
    user_peers = lax.axis_size("user")
    item_peers = lax.axis_size("item")
    user_index = tile_user[0, 0]
    item_index = tile_item[0, 0]
    slot_count = user_index.shape[1]
    live_slots = (
        jnp.arange(slot_count, dtype=jnp.int32)[None, :] < tile_count[0, 0][:, None]
    ).astype(jnp.int32)
    confidence = tile_conf[0, 0]
    whole_users = lax.all_gather(user_factors, "user", axis=0, tiled=True)
    gram_users = lax.psum(local_gram(user_factors), "user")
    user_table = whole_users.reshape(user_peers, -1, tile_width, factor_rank)
    tile_factors = user_table[jnp.arange(user_peers, dtype=jnp.int32)[:, None], user_index]
    factors = tile_factors.reshape(-1, tile_width, factor_rank)
    weights, right_weights = tile_weights(confidence, live_slots, tile_width)
    item_blocks = item_factors.shape[0] // tile_width
    positions = item_index.reshape(-1)
    onehot = block_onehot(positions, item_blocks)
    warm_start = item_factors.reshape(item_blocks, tile_width, factor_rank)

    def item_operator(direction):
        return user_total(item_terms(factors, weights, positions, onehot, direction)) + gram_apply(
            direction, gram_users
        )

    start_total = user_total(
        item_right(factors, right_weights, onehot)
        - item_terms(factors, weights, positions, onehot, warm_start)
    )
    residual = start_total - gram_apply(warm_start, gram_users)
    own_items = conjugate(item_operator, residual, warm_start)
    new_items = own_items.reshape(-1, factor_rank)
    held_index = held_user[0, 0]
    owner_index = held_item[0, 0]
    held_slots = owner_index.shape[1]
    held_live = (
        jnp.arange(held_slots, dtype=jnp.int32)[None, :] < held_count[0, 0][:, None]
    ).astype(jnp.int32)
    held_confidence = held_conf[0, 0]
    whole_items = lax.all_gather(new_items, "item", axis=0, tiled=True)
    gram_items = lax.psum(local_gram(new_items), "item")
    item_table = whole_items.reshape(item_peers, -1, tile_width, factor_rank)
    held_factors = item_table[jnp.arange(item_peers, dtype=jnp.int32)[:, None], owner_index]
    held_flat = held_factors.reshape(-1, tile_width, factor_rank)
    held_weights, held_right_weights = tile_weights(held_confidence, held_live, tile_width)
    held_positions = held_index.reshape(-1)
    held_onehot = block_onehot(held_positions, HB_DEV)

    def held_operator(direction):
        return item_total(
            held_terms(held_flat, held_weights, held_positions, held_onehot, direction)
        ) + gram_apply(direction, gram_items)

    held_residual = item_total(held_right(held_flat, held_right_weights, held_onehot))
    zero_start = jnp.zeros((HB_DEV, tile_width, factor_rank), jnp.float32)
    folded_users = conjugate(held_operator, held_residual, zero_start).reshape(-1, factor_rank)
    return (new_items, folded_users)


def solution(mesh):
    in_specs = (
        P("user", None),
        P("item", None),
        P("item", "user", None, None),
        P("item", "user", None, None),
        P("item", "user", None),
        P("item", "user", None, None, None, None),
        P("user", "item", None, None),
        P("user", "item", None, None),
        P("user", "item", None),
        P("user", "item", None, None, None, None),
    )
    out_specs = (P("item", None), P("user", None))
    return jax.shard_map(shards, mesh=mesh, in_specs=in_specs, out_specs=out_specs, check_vma=False)
```

profile of v0, /device:TPU:2, one launch (start us, length us, event | category | flops | bytes accessed | tf_op | source)
XLA Modules:
  0.0 905.1 jit_solution(9983996490653584908)
XLA Ops:
  10.6 3.8 gather_fusion.1
  16.2 52.5 %all-gather.3.cloned.1.call-done = f32[8192,256]{1,0:T(8,128)} async-done(((f32[512,256]{1,0:T(8,128)}), f32[8192,256]{1,0:T(8,128)}) %all-gather.3.cloned.1.call-update) | async-done | bytes 8388624 | tf_op jit(solution)/shard_map/all_gather | solution.py:101
  68.7 6.1 gather_fusion
  74.9 8.0 fusion.80
  82.9 4.5 fusion.30
  87.3 4.7 fusion.23
  92.1 3.8 fusion.10
  95.9 3.8 fusion.12
  101.2 109.1 %all-reduce.19.cloned.1.call-done = (f32[4,128,256]{2,1,0:T(8,128)}, f32[256,256]{1,0:T(8,128)}) async-done(((f32[4,128,256]{2,1,0:T(8,128)}, f32[256,256]{1,0:T(8,128)}), (f32[4,128,256]{2,1,0:T(8,128)}, f32[256,256]{1,0:T(8,128)})) %all-reduce.19.cloned.1.call-update) | async-done | bytes 786448 | tf_op jit(solution)/shard_map/psum | solution.py:65
  214.8 8.0 fusion.82
  222.8 4.5 fusion.25
  227.4 4.0 fusion.8
  232.3 110.0 %all-reduce.9.cloned.1.call-done = f32[4,128,256]{2,1,0:T(8,128)} async-done(((f32[4,128,256]{2,1,0:T(8,128)}), f32[4,128,256]{2,1,0:T(8,128)}) %all-reduce.9.cloned.1.call-update) | async-done | bytes 524304 | tf_op jit(solution)/shard_map/psum | solution.py:65
  344.5 2.8 gather_fusion.3
  347.3 8.0 fusion.83
  355.3 4.5 fusion.27
  359.9 4.0 fusion.6
  364.9 109.9 %all-reduce.11.cloned.1.call-done = f32[4,128,256]{2,1,0:T(8,128)} async-done(((f32[4,128,256]{2,1,0:T(8,128)}), f32[4,128,256]{2,1,0:T(8,128)}) %all-reduce.11.cloned.1.call-update) | async-done | bytes 524304 | tf_op jit(solution)/shard_map/psum | solution.py:65
  478.2 75.8 %all-gather.5.cloned.1.call-done = f32[8192,256]{1,0:T(8,128)} async-done(((f32[512,256]{1,0:T(8,128)}), f32[8192,256]{1,0:T(8,128)}) %all-gather.5.cloned.1.call-update) | async-done | bytes 8388624 | tf_op jit(solution)/shard_map/all_gather | solution.py:131
  554.0 6.2 gather_fusion.4
  560.3 5.6 fusion.33
  565.9 3.8 fusion.4
  572.7 91.6 %all-reduce.13.cloned.1.call-done = f32[2,128,256]{2,1,0:T(8,128)} async-done(((f32[2,128,256]{2,1,0:T(8,128)}), f32[2,128,256]{2,1,0:T(8,128)}) %all-reduce.13.cloned.1.call-update) | async-done | bytes 262160 | tf_op jit(solution)/shard_map/psum | solution.py:69
  664.3 3.7 gather_fusion.5
  668.0 8.0 fusion.84
  676.0 4.5 fusion.19
  680.5 4.0 fusion.2
  685.3 94.8 %all-reduce.17.cloned.1.call-done = (f32[2,128,256]{2,1,0:T(8,128)}, f32[256,256]{1,0:T(8,128)}) async-done(((f32[2,128,256]{2,1,0:T(8,128)}, f32[256,256]{1,0:T(8,128)}), (f32[2,128,256]{2,1,0:T(8,128)}, f32[256,256]{1,0:T(8,128)})) %all-reduce.17.cloned.1.call-update) | async-done | bytes 524304 | tf_op jit(solution)/shard_map/psum | solution.py:69
  784.8 8.0 fusion.85
  792.8 4.5 fusion.21
  797.3 3.8 fusion
  801.9 93.9 %all-reduce.15.cloned.1.call-done = f32[2,128,256]{2,1,0:T(8,128)} async-done(((f32[2,128,256]{2,1,0:T(8,128)}), f32[2,128,256]{2,1,0:T(8,128)}) %all-reduce.15.cloned.1.call-update) | async-done | bytes 262160 | tf_op jit(solution)/shard_map/psum | solution.py:69
  (95 shorter events, 30.0 us)
Async XLA Ops:
  7.2 61.6 %all-gather.3.cloned.1.call-start = ((), (), s32[]{:S(2)}) async-start(), calls=%async_computation | async-start | bytes 8912896 | tf_op jit(solution)/shard_map/all_gather | solution.py:101
  7.9 202.4 %all-reduce.19.cloned.1.call-start = ((), (), s32[]{:S(2)}) async-start(), calls=%async_computation.7 | async-start | bytes 1572864 | tf_op jit(solution)/shard_map/psum | solution.py:65
  10.6 3.9 copy-start.10
  74.9 8.0 copy-start
  74.9 8.0 copy-start.7
  95.9 114.4 %copy-start.6 = (f32[512,256]{1,0:T(8,128)S(1)}, f32[512,256]{1,0:T(8,128)}, u32[]{:S(2)}) copy-start(f32[512,256]{1,0:T(8,128)} %param.11) | copy-start | bytes 1572868
  100.7 241.6 %all-reduce.9.cloned.1.call-start = ((), (), s32[]{:S(2)}) async-start(), calls=%async_computation.1 | async-start | bytes 1048576 | tf_op jit(solution)/shard_map/psum | solution.py:65
  214.8 8.0 copy-start.1
  227.4 114.9 %copy-start.11 = (f32[256,256]{1,0:T(8,128)S(1)}, f32[256,256]{1,0:T(8,128)}, u32[]{:S(2)}) copy-start(f32[256,256]{1,0:T(8,128)} %get-tuple-element.9) | copy-start | bytes 786436
  232.3 242.5 %all-reduce.11.cloned.1.call-start = ((), (), s32[]{:S(2)}) async-start(), calls=%async_computation.2 | async-start | bytes 1048576 | tf_op jit(solution)/shard_map/psum | solution.py:65
  347.3 8.0 copy-start.2
  359.8 117.7 %copy-start.13 = (s32[1,1,16,2]{2,3,1,0:T(2,128)S(1)}, s32[1,1,16,2]{2,3,1,0:T(2,128)}, u32[]{:S(2)}) copy-start(s32[1,1,16,2]{2,3,1,0:T(2,128)} %param.16) | copy-start | bytes 388
  359.9 118.0 %copy-start.14 = (s32[1,1,16,2]{2,3,1,0:T(2,128)S(1)}, s32[1,1,16,2]{2,3,1,0:T(2,128)}, u32[]{:S(2)}) copy-start(s32[1,1,16,2]{2,3,1,0:T(2,128)} %param.17) | copy-start | bytes 388
  359.9 118.2 %copy-start.15 = (s32[1,1,16]{2,1,0:T(1,128)S(1)}, s32[1,1,16]{2,1,0:T(1,128)}, u32[]{:S(2)}) copy-start(s32[1,1,16]{2,1,0:T(1,128)} %param.18) | copy-start | bytes 196
  364.8 189.2 %all-gather.5.cloned.1.call-start = ((), (), s32[]{:S(2)}) async-start(), calls=%async_computation.3 | async-start | bytes 8912896 | tf_op jit(solution)/shard_map/all_gather | solution.py:131
  477.5 186.8 %all-reduce.13.cloned.1.call-start = ((), (), s32[]{:S(2)}) async-start(), calls=%async_computation.4 | async-start | bytes 524288 | tf_op jit(solution)/shard_map/psum | solution.py:69
  554.0 6.2 copy-start.8
  565.9 5.1 copy-start.9
  570.5 209.7 %all-reduce.17.cloned.1.call-start = ((), (), s32[]{:S(2)}) async-start(), calls=%async_computation.6 | async-start | bytes 1048576 | tf_op jit(solution)/shard_map/psum | solution.py:69
  668.0 8.0 copy-start.3
  680.5 99.6 %copy-start.5 = (f32[2,128,256]{2,1,0:T(8,128)S(1)}, f32[2,128,256]{2,1,0:T(8,128)}, u32[]{:S(2)}) copy-start(f32[2,128,256]{2,1,0:T(8,128)} %all-reduce.13.cloned.1.call-done) | copy-start | bytes 786436
  685.3 210.5 %all-reduce.15.cloned.1.call-start = ((), (), s32[]{:S(2)}) async-start(), calls=%async_computation.5 | async-start | bytes 524288 | tf_op jit(solution)/shard_map/psum | solution.py:69
  784.8 8.0 copy-start.4
  797.3 98.5 %copy-start.12 = (f32[256,256]{1,0:T(8,128)S(1)}, f32[256,256]{1,0:T(8,128)}, u32[]{:S(2)}) copy-start(f32[256,256]{1,0:T(8,128)} %get-tuple-element.7) | copy-start | bytes 786436
Sparse Core Ops, SparseCore 0:
  9.8 58.8 all-gather.2
  100.8 109.4 all-reduce.18
  232.4 109.8 all-reduce.8
  364.9 109.7 all-reduce.10
  477.9 76.0 all-gather.4
  570.6 93.7 all-reduce.12
  685.4 94.7 all-reduce.16
  802.0 93.7 all-reduce.14
where the time goes:
time: 914 us; the launch traced here: 905 us
  waiting for transfers between devices  738 us (81%)
  matrix products  112 us (12%)
  local copies, waits for them, and re-layouts  33.9 us (4%)
  between operations  14.7 us (2%)
    psum x3, waiting for transfers between devices, user_total(): return lax.psum(partial_value, 'user')  329 us
    psum x3, waiting for transfers between devices, item_total(): return lax.psum(partial_value, 'item')  280 us
    all_gather x1, waiting for transfers between devices, shards(): whole_items = lax.all_gather(new_items, 'item', axis=0, tiled=True)  75.8 us
    all_gather x1, waiting for transfers between devices, shards(): whole_users = lax.all_gather(user_factors, 'user', axis=0, tiled=True)  52.5 us
    dot_general x3, matrix products, item_terms(): jnp.einsum('tuk,tik->tui', factors, picked, precision=highest) * weights  24 us
  transfers between devices with their start and end apart: 8, of which 8 were waited for; matrix products, arithmetic and copies ran while one was open for 1% of the time, Pallas kernels for 0%

commit v1 on v0

--- a/solution.py
+++ b/solution.py
@@ -98,7 +98,9 @@
         jnp.arange(slot_count, dtype=jnp.int32)[None, :] < tile_count[0, 0][:, None]
     ).astype(jnp.int32)
     confidence = tile_conf[0, 0]
-    whole_users = lax.all_gather(user_factors, "user", axis=0, tiled=True)
+    whole_users = jnp.concatenate(
+        lax.all_to_all(jnp.stack([user_factors] * lax.axis_size("user")), "user", 0, 0), axis=0
+    )
     gram_users = lax.psum(local_gram(user_factors), "user")
     user_table = whole_users.reshape(user_peers, -1, tile_width, factor_rank)
     tile_factors = user_table[jnp.arange(user_peers, dtype=jnp.int32)[:, None], user_index]

time: 914 us -> 1050 us (1.15)
  waiting for transfers between devices: 738 us -> 865 us
    all_to_all x0 -> x1, waiting for transfers between devices: none -> 179 us  [shards(): lax.all_to_all(jnp.stack([user_factors] * lax.axis_size('user')), 'user',...]
    all_gather x1 -> x0, waiting for transfers between devices: 52.5 us -> none  [shards(): whole_users = lax.all_gather(user_factors, 'user', axis=0, tiled=True)]
where the time goes in v1:
time: 1050 us; the launch traced here: 1040 us
  waiting for transfers between devices  865 us (82%)
  matrix products  112 us (11%)
  local copies, waits for them, and re-layouts  37.3 us (4%)
  between operations  14.7 us (1%)
    psum x3, waiting for transfers between devices, user_total(): return lax.psum(partial_value, 'user')  330 us
    psum x3, waiting for transfers between devices, item_total(): return lax.psum(partial_value, 'item')  280 us
    all_to_all x1, waiting for transfers between devices, shards(): lax.all_to_all(jnp.stack([user_factors] * lax.axis_size('user')), 'user',...  179 us
    all_gather x1, waiting for transfers between devices, shards(): whole_items = lax.all_gather(new_items, 'item', axis=0, tiled=True)  75.8 us
    dot_general x3, matrix products, item_terms(): jnp.einsum('tuk,tik->tui', factors, picked, precision=highest) * weights  24 us
  transfers between devices with their start and end apart: 8, of which 8 were waited for; matrix products, arithmetic and copies ran while one was open for 1% of the time, Pallas kernels for 0%

profile of v1, /device:TPU:2, one launch (start us, length us, event | category | flops | bytes accessed | tf_op | source)
XLA Modules:
  0.0 1042.6 jit_solution(2107763533154759950)
XLA Ops:
  7.2 5.1 stack.2
  12.3 8.8 all-to-all-start
  26.3 179.0 %all-to-all-done = f32[16,512,256]{2,1,0:T(8,128)} async-done(((f32[16,512,256]{2,1,0:T(8,128)}), f32[16,512,256]{2,1,0:T(8,128)}, u32[]{:S(2)}, u32[]{:S(2)}) %all-to-all-start) | async-done | bytes 8388640 | tf_op jit(solution)/shard_map/all_to_all | solution.py:102
  205.3 6.2 gather_fusion
  211.4 8.0 fusion.80
  219.5 4.5 fusion.30
  223.9 4.7 fusion.23
  228.7 3.8 fusion.10
  232.5 3.8 fusion.12
  237.8 109.8 %all-reduce.19.cloned.1.call-done = (f32[4,128,256]{2,1,0:T(8,128)}, f32[256,256]{1,0:T(8,128)}) async-done(((f32[4,128,256]{2,1,0:T(8,128)}, f32[256,256]{1,0:T(8,128)}), (f32[4,128,256]{2,1,0:T(8,128)}, f32[256,256]{1,0:T(8,128)})) %all-reduce.19.cloned.1.call-update) | async-done | bytes 786448 | tf_op jit(solution)/shard_map/psum | solution.py:65
  352.1 8.0 fusion.82
  360.1 4.5 fusion.25
  364.6 4.0 fusion.8
  369.6 110.0 %all-reduce.9.cloned.1.call-done = f32[4,128,256]{2,1,0:T(8,128)} async-done(((f32[4,128,256]{2,1,0:T(8,128)}), f32[4,128,256]{2,1,0:T(8,128)}) %all-reduce.9.cloned.1.call-update) | async-done | bytes 524304 | tf_op jit(solution)/shard_map/psum | solution.py:65
  484.6 8.0 fusion.83
  492.6 4.5 fusion.27
  497.2 4.0 fusion.6
  502.2 110.1 %all-reduce.11.cloned.1.call-done = f32[4,128,256]{2,1,0:T(8,128)} async-done(((f32[4,128,256]{2,1,0:T(8,128)}), f32[4,128,256]{2,1,0:T(8,128)}) %all-reduce.11.cloned.1.call-update) | async-done | bytes 524304 | tf_op jit(solution)/shard_map/psum | solution.py:65
  615.7 75.8 %all-gather.2.cloned.1.call-done = f32[8192,256]{1,0:T(8,128)} async-done(((f32[512,256]{1,0:T(8,128)}), f32[8192,256]{1,0:T(8,128)}) %all-gather.2.cloned.1.call-update) | async-done | bytes 8388624 | tf_op jit(solution)/shard_map/all_gather | solution.py:133
  691.5 6.3 gather_fusion.4
  697.8 5.6 fusion.33
  703.4 3.8 fusion.4
  710.2 91.6 %all-reduce.13.cloned.1.call-done = f32[2,128,256]{2,1,0:T(8,128)} async-done(((f32[2,128,256]{2,1,0:T(8,128)}), f32[2,128,256]{2,1,0:T(8,128)}) %all-reduce.13.cloned.1.call-update) | async-done | bytes 262160 | tf_op jit(solution)/shard_map/psum | solution.py:69
  801.8 3.7 gather_fusion.5
  805.5 8.0 fusion.84
  813.5 4.5 fusion.19
  818.0 4.0 fusion.2
  822.8 94.8 %all-reduce.17.cloned.1.call-done = (f32[2,128,256]{2,1,0:T(8,128)}, f32[256,256]{1,0:T(8,128)}) async-done(((f32[2,128,256]{2,1,0:T(8,128)}, f32[256,256]{1,0:T(8,128)}), (f32[2,128,256]{2,1,0:T(8,128)}, f32[256,256]{1,0:T(8,128)})) %all-reduce.17.cloned.1.call-update) | async-done | bytes 524304 | tf_op jit(solution)/shard_map/psum | solution.py:69
  922.3 8.0 fusion.85
  930.3 4.5 fusion.21
  934.8 3.8 fusion
  939.4 93.9 %all-reduce.15.cloned.1.call-done = f32[2,128,256]{2,1,0:T(8,128)} async-done(((f32[2,128,256]{2,1,0:T(8,128)}), f32[2,128,256]{2,1,0:T(8,128)}) %all-reduce.15.cloned.1.call-update) | async-done | bytes 262160 | tf_op jit(solution)/shard_map/psum | solution.py:69
  (101 shorter events, 32.8 us)
Async XLA Ops:
  12.2 8.8 copy-start.13
  12.2 9.1 copy-start.15
  12.2 9.3 copy-start.17
  12.3 9.5 copy-start.6
  12.3 193.0 %all-to-all-start = ((f32[16,512,256]{2,1,0:T(8,128)}), f32[16,512,256]{2,1,0:T(8,128)}, u32[]{:S(2)}, u32[]{:S(2)}) async-start(f32[16,512,256]{2,1,0:T(8,128)} %stack.2), calls=%async_computation | async-start | bytes 16777216 | tf_op jit(solution)/shard_map/all_to_all | solution.py:102
  21.0 326.6 %all-reduce.19.cloned.1.call-start = ((), (), s32[]{:S(2)}) async-start(), calls=%async_computation.7 | async-start | bytes 1572864 | tf_op jit(solution)/shard_map/psum | solution.py:65
  21.8 2.8 copy-start.10
  211.4 8.0 copy-start
  211.4 8.0 copy-start.7
  237.3 242.3 %all-reduce.9.cloned.1.call-start = ((), (), s32[]{:S(2)}) async-start(), calls=%async_computation.1 | async-start | bytes 1048576 | tf_op jit(solution)/shard_map/psum | solution.py:65
  352.1 8.0 copy-start.1
  364.6 114.9 %copy-start.11 = (f32[256,256]{1,0:T(8,128)S(1)}, f32[256,256]{1,0:T(8,128)}, u32[]{:S(2)}) copy-start(f32[256,256]{1,0:T(8,128)} %get-tuple-element.9) | copy-start | bytes 786436
  369.5 242.7 %all-reduce.11.cloned.1.call-start = ((), (), s32[]{:S(2)}) async-start(), calls=%async_computation.2 | async-start | bytes 1048576 | tf_op jit(solution)/shard_map/psum | solution.py:65
  484.6 8.0 copy-start.2
  497.1 117.9 %copy-start.14 = (s32[1,1,16,2]{2,3,1,0:T(2,128)S(1)}, s32[1,1,16,2]{2,3,1,0:T(2,128)}, u32[]{:S(2)}) copy-start(s32[1,1,16,2]{2,3,1,0:T(2,128)} %param.16) | copy-start | bytes 388
  497.1 118.2 %copy-start.16 = (s32[1,1,16,2]{2,3,1,0:T(2,128)S(1)}, s32[1,1,16,2]{2,3,1,0:T(2,128)}, u32[]{:S(2)}) copy-start(s32[1,1,16,2]{2,3,1,0:T(2,128)} %param.17) | copy-start | bytes 388
  497.2 118.3 %copy-start.18 = (s32[1,1,16]{2,1,0:T(1,128)S(1)}, s32[1,1,16]{2,1,0:T(1,128)}, u32[]{:S(2)}) copy-start(s32[1,1,16]{2,1,0:T(1,128)} %param.18) | copy-start | bytes 196
  502.1 189.4 %all-gather.2.cloned.1.call-start = ((), (), s32[]{:S(2)}) async-start(), calls=%async_computation.3 | async-start | bytes 8912896 | tf_op jit(solution)/shard_map/all_gather | solution.py:133
  615.0 186.8 %all-reduce.13.cloned.1.call-start = ((), (), s32[]{:S(2)}) async-start(), calls=%async_computation.4 | async-start | bytes 524288 | tf_op jit(solution)/shard_map/psum | solution.py:69
  691.5 6.3 copy-start.8
  703.4 5.1 copy-start.9
  707.9 209.7 %all-reduce.17.cloned.1.call-start = ((), (), s32[]{:S(2)}) async-start(), calls=%async_computation.6 | async-start | bytes 1048576 | tf_op jit(solution)/shard_map/psum | solution.py:69
  805.5 8.0 copy-start.3
  818.0 99.6 %copy-start.5 = (f32[2,128,256]{2,1,0:T(8,128)S(1)}, f32[2,128,256]{2,1,0:T(8,128)}, u32[]{:S(2)}) copy-start(f32[2,128,256]{2,1,0:T(8,128)} %all-reduce.13.cloned.1.call-done) | copy-start | bytes 786436
  822.8 210.5 %all-reduce.15.cloned.1.call-start = ((), (), s32[]{:S(2)}) async-start(), calls=%async_computation.5 | async-start | bytes 524288 | tf_op jit(solution)/shard_map/psum | solution.py:69
  922.3 8.0 copy-start.4
  934.8 98.4 %copy-start.12 = (f32[256,256]{1,0:T(8,128)S(1)}, f32[256,256]{1,0:T(8,128)}, u32[]{:S(2)}) copy-start(f32[256,256]{1,0:T(8,128)} %get-tuple-element.7) | copy-start | bytes 786436
Sparse Core Ops, SparseCore 0:
  237.4 110.1 all-reduce.18
  369.7 109.8 all-reduce.8
  502.2 109.9 all-reduce.10
  615.4 76.0 all-gather.1
  708.1 93.7 all-reduce.12
  822.9 94.7 all-reduce.16
  939.5 93.7 all-reduce.14
